TPU v7x, 128 devices: a whole 4x4x4 slice. The times are simulated.
128 devices in a mesh: doc: 2 (over core), coarse: 4 (over z), fine: 16 (over y, x).
Axes of the slice: x: 4, y: 4, z: 4, core: 2. Of those that a mesh axis runs over, the one named last changes fastest.
Arguments:
- q_light: bfloat16 [2, 8192, 1024], P('doc', ('coarse', 'fine')), may hold values from -8 to 8
- k_light: bfloat16 [2, 8192, 1024], P('doc', ('coarse', 'fine')), may hold values from -8 to 8
- v_light: bfloat16 [2, 8192, 1024], P('doc', ('coarse', 'fine')), may hold values from -6 to 6
- q_heavy: bfloat16 [2, 8192, 1024], P('doc', ('coarse', 'fine')), may hold values from -8 to 8
- k_heavy: bfloat16 [2, 8192, 1024], P('doc', ('coarse', 'fine')), may hold values from -8 to 8
- v_heavy: bfloat16 [2, 8192, 1024], P('doc', ('coarse', 'fine')), may hold values from -6 to 6
- enc_kv: bfloat16 [2, 8192, 128], P('doc', ('coarse', 'fine')), may hold values from -8 to 8
- dec_queries: bfloat16 [2, 512, 1024], P('doc'), may hold values from -8 to 8
- query_ids: int32 [2, 64], P('doc'), may hold values from 0 to 63, as said below
- key_ids: int32 [2, 32], P('doc'), may hold values from 0 to 63, as said below
Outputs:
- encoded: bfloat16 [2, 8192, 1024], P('doc', ('coarse', 'fine'))
- decoded: bfloat16 [2, 512, 1024], P('doc')
Inputs may be any that keep to these rules, and one draw needn't show every extreme that they name: `query_ids`: for each document and each c below the number of coarse groups, entries c * 16 to (c + 1) * 16 - 1 are distinct block numbers among blocks c * 16 to (c + 1) * 16 - 1 (so every block of the group is listed), and entry c * 16 + f is the block assigned to the f-th device of that group. `key_ids`: for each document and each c below the number of coarse groups, entries c * 8 to (c + 1) * 8 - 1 are distinct block numbers among blocks c * 16 * 1 to (c + 1) * 16 - 1.
All inputs are finite; a program needn't handle non-finite values.
Results may differ from a plain program's by a relative error of at most 0.009.
Values may be sent and summed in bfloat16 or wider, within the bound.
No kernel may reach another device: no remote copies, remote signals or barrier semaphores. Data moves between devices by JAX's collectives and lax.ppermute only.
A program may use at most 384 MiB of HBM per device.

v0:
```python
import jax
import jax.numpy as jnp
from jax import lax
from jax.sharding import Mesh
from jax.sharding import PartitionSpec as P

HEAD = 64
ROUTED_BLOCK = 128
KGRP = 8
COARSE_FINE = ("coarse", "fine_0", "fine_1")
FINE = ("fine_0", "fine_1")


def extended(value, sides, width):
    edges = {}
    for axis, dim in sides:
        size, length = (lax.axis_size(axis), value.shape[dim])
        up = [(i, (i + 1) % size) for i in range(size - 1)]
        last = lax.slice_in_dim(value, length - width, length, axis=dim)
        first = lax.slice_in_dim(value, 0, width, axis=dim)
        edges[dim] = (
            lax.ppermute(last, axis, up),
            lax.ppermute(first, axis, [(b, a) for a, b in up]),
        )
    done = []
    for _, dim in sides:
        low, high = edges[dim]
        around = [(width, width) if d in done else (0, 0) for d in range(value.ndim)]
        value = jnp.concatenate([jnp.pad(low, around), value, jnp.pad(high, around)], axis=dim)
        done.append(dim)
    return value


def split_up(value, dim, length):
    lengths = value.shape
    pieces = value.reshape(*lengths[:dim], length, lengths[dim] // length, *lengths[dim + 1 :])
    return jnp.moveaxis(pieces, dim, 0)


def sum_at_owner(value, axis, dim):
    pieces = split_up(value, dim, lax.axis_size(axis))
    arrived = lax.all_to_all(pieces, axis, split_axis=0, concat_axis=0, tiled=True)
    return arrived.astype(jnp.float32).sum(axis=0)


def joined_all(value, axes, combine):
    for axis in axes:
        pieces = jax.tree.map(lambda part: lax.all_gather(part, axis), value)
        value = jax.tree.map(lambda part: part[0], pieces)
        for k in range(1, lax.axis_size(axis)):
            value = combine(value, jax.tree.map(lambda part: part[k], pieces))
    return value


def attend(query, keys, value_rows, mask):
    rows = query.shape[0]
    count = keys.shape[0]
    heads = query.shape[1] // HEAD
    qh = query.reshape(rows, heads, HEAD).transpose(1, 0, 2)
    kh = keys.reshape(count, heads, HEAD).transpose(1, 0, 2)
    vh = value_rows.reshape(count, heads, HEAD).transpose(1, 0, 2)

    def one_head(triple):
        qa, ka, va = triple
        scores = jnp.dot(qa, ka.T, preferred_element_type=jnp.float32) * HEAD ** (-0.5)
        if mask is not None:
            scores = jnp.where(mask, scores, jnp.float32(-1e30))
        peak = jnp.max(scores, axis=1, keepdims=True)
        weights = jnp.exp(scores - peak)
        weights = (weights / jnp.sum(weights, axis=1, keepdims=True)).astype(jnp.bfloat16)
        return jnp.dot(weights, va, preferred_element_type=jnp.float32)

    out = lax.map(one_head, (qh, kh, vh))
    return out.transpose(1, 0, 2).reshape(rows, heads * HEAD)


def combine(leading_entry, second):
    peak = jnp.maximum(leading_entry[0], second[0])
    scale_a = jnp.exp(leading_entry[0] - peak)
    scale_b = jnp.exp(second[0] - peak)
    total = leading_entry[1] * scale_a + second[1] * scale_b
    value_rows = leading_entry[2] * scale_a[..., None] + second[2] * scale_b[..., None]
    return (peak, total, value_rows)


def local(
    q_light, k_light, v_light, q_heavy, k_heavy, v_heavy, enc_kv, dec_queries, query_ids, key_ids
):
    query = q_light[0]
    tokens, width = query.shape
    n_seq = lax.axis_size(COARSE_FINE)
    n_fine = lax.axis_size(FINE)
    here = lax.axis_index(COARSE_FINE)
    group = lax.axis_index("coarse")
    start = here * tokens
    light_kv = jnp.concatenate([k_light[0], v_light[0]], axis=1)
    padded = extended(light_kv, ((COARSE_FINE, 0),), ROUTED_BLOCK)
    key_pos = start - ROUTED_BLOCK + jnp.arange(tokens + 2 * ROUTED_BLOCK, dtype=jnp.int32)
    inside = (key_pos >= 0) & (key_pos < tokens * n_seq)
    rows = min(512, tokens)
    qpos = start + 0 + jnp.arange(rows, dtype=jnp.int32)
    mask = (jnp.abs(qpos[:, None] - key_pos[None, :]) <= ROUTED_BLOCK - 1) & inside[None, :]
    pieces = attend(query, padded[:, :width], padded[:, width:], mask)
    blocks = tokens // ROUTED_BLOCK
    mine = here * blocks + jnp.arange(blocks, dtype=jnp.int32)
    key_group = lax.dynamic_slice_in_dim(key_ids[0], group * KGRP, KGRP)
    pick_keys = (key_group[:, None] == mine[None, :]).astype(jnp.bfloat16)
    heavy_kv = jnp.concatenate([k_heavy[0], v_heavy[0]], axis=1).reshape(
        blocks, ROUTED_BLOCK, 2 * width
    )
    slots = jnp.einsum(
        "sb,bre->sre", pick_keys, heavy_kv, preferred_element_type=jnp.float32
    ).reshape(KGRP * ROUTED_BLOCK, 2 * width)
    share = sum_at_owner(slots.astype(jnp.bfloat16), FINE, 0).astype(jnp.bfloat16)
    keys_all = lax.all_gather(share, COARSE_FINE, axis=0, tiled=True)
    query_group = lax.dynamic_slice_in_dim(query_ids[0], group * n_fine, n_fine)
    pick_rows = (query_group[:, None] == mine[None, :]).astype(jnp.bfloat16)
    heavy_query = q_heavy[0]
    result = attend(heavy_query, keys_all[:, :width], keys_all[:, width:], None).astype(
        jnp.bfloat16
    )
    chosen = jnp.sum(pick_rows.astype(jnp.float32), axis=0)
    heavy = (
        result.reshape(blocks, ROUTED_BLOCK, width).astype(jnp.float32) * chosen[:, None, None]
    ).reshape(tokens, width)
    encoded = (pieces + heavy).astype(jnp.bfloat16)[None]
    decoder_query_rows = dec_queries[0]
    count = decoder_query_rows.shape[0]
    heads = width // HEAD
    enc_keys = enc_kv[0][:, :HEAD]
    enc_values = enc_kv[0][:, HEAD:]
    heads_query = decoder_query_rows.reshape(count, heads, HEAD).transpose(1, 0, 2)

    def partial_head(qa):
        scores = jnp.dot(qa, enc_keys.T, preferred_element_type=jnp.float32) * HEAD ** (-0.5)
        peak = jnp.max(scores, axis=1)
        weights = jnp.exp(scores - peak[:, None])
        total = jnp.sum(weights, axis=1)
        value_rows = jnp.dot(
            weights.astype(jnp.bfloat16), enc_values, preferred_element_type=jnp.float32
        )
        return (peak, total, value_rows)

    peak, total, value_rows = lax.map(partial_head, heads_query)
    peak, total, value_rows = joined_all((peak, total, value_rows), COARSE_FINE, combine)
    decoded = (
        (value_rows / total[..., None])
        .transpose(1, 0, 2)
        .reshape(count, width)
        .astype(jnp.bfloat16)[None]
    )
    return (encoded, decoded)


def solution(mesh):
    torus = Mesh(
        mesh.devices.reshape(mesh.shape["doc"], mesh.shape["coarse"], 4, 4),
        ("doc", "coarse", "fine_0", "fine_1"),
    )
    return jax.shard_map(
        local,
        mesh=torus,
        in_specs=(
            P("doc", COARSE_FINE, None),
            P("doc", COARSE_FINE, None),
            P("doc", COARSE_FINE, None),
            P("doc", COARSE_FINE, None),
            P("doc", COARSE_FINE, None),
            P("doc", COARSE_FINE, None),
            P("doc", COARSE_FINE, None),
            P("doc", None, None),
            P("doc", None),
            P("doc", None),
        ),
        out_specs=(P("doc", COARSE_FINE, None), P("doc", None, None)),
        check_vma=False,
    )
```

profile of v0, /device:TPU:1, one launch (start us, length us, event | category | flops | bytes accessed | tf_op | source)
XLA Modules:
  0.0 475.2 jit_solution(11982831535126823827)
XLA Ops:
  7.2 1.5 copy.56
  8.8 19.9 %while.39 = (s32[]{:T(128)}, f32[16,512]{1,0:T(8,128)S(1)}, f32[16,512]{1,0:T(8,128)S(1)}, f32[16,512,64]{1,2,0:T(8,128)}, bf16[16,512,64]{1,2,0:T(8,128)(2,1)S(...) while((s32[]{:T(128)}, f32[16,512]{1,0:T(8,128)S(1)}, ...), condition=%wide.region_13.14_spmd.clone, body=%wide.region_10.13_spmd.sunk.clone | while | flops 17169408 | bytes 1048677 | solution.py:144
  28.9 11.6 %all-gather.1 = f32[64,512]{1,0:T(8,128)S(1)} all-gather(f32[16,512]{1,0:T(8,128)S(1)} %get-tuple-element.103), channel_id=3, replica_groups=mesh['doc'=2,'coarse'=4,'fine_0'=4,'fine_1'=4] {'coarse'}, dimensions={0}, use_global_device_ids=true | all-gather | bytes 163840 | tf_op jit(solution)/shard_map/all_gather | solution.py:48
  40.5 75.0 %all-gather.14.cloned.1.call-done = f32[64,512,64]{1,2,0:T(8,128)} async-done(((f32[16,512,64]{1,2,0:T(8,128)}), f32[64,512,64]{1,2,0:T(8,128)}) %all-gather.14.cloned.1.call-update) | async-done | bytes 8388624 | tf_op jit(solution)/shard_map/all_gather | solution.py:48
  115.5 6.3 %fusion.50 = f32[1,16,512,64]{2,3,1,0:T(8,128)} fusion(f32[64,512,64]{1,2,0:T(8,128)} %all-gather.14.cloned.1.call-done, f32[16,512]{1,0:T(8,128)S(1)} %get-tuple-element.266, f32[16,512]{1,0:T(8,128)S(1)} %get-tuple-element.263, f32[16,512]{1,0:T(8,128)S(1)} %get-tuple-element.265, f32[16,512]{1,0:T(8,128)S(1)} %get-tuple-element.264, ...), kind=kLoop, calls=%fused_computation.70 | loop fusion | flops 4718592 | bytes 10682368 | tf_op jit(solution)/shard_map/add | solution.py:82
  123.0 1.2 multiply_convert_fusion
  124.2 61.8 %all_to_all.5 = bf16[16,64,2048]{2,1,0:T(8,128)(2,1)} all-to-all(bf16[16,64,2048]{2,1,0:T(8,128)(2,1)S(1)} %bitcast.387), channel_id=1, replica_groups=mesh['doc'=2,'coarse'=4,'fine_0'=4,'fine_1'=4] {'fine_0','fine_1'}, dimensions={0} | all-to-all | bytes 8388608 | tf_op jit(solution)/shard_map/all_to_all | solution.py:42
  185.9 3.9 reduce_sum.48
  190.3 1.3 collective-permute-start.1
  191.6 5.0 %collective-permute-start = (bf16[128,2048]{0,1:T(8,128)(2,1)S(1)}, bf16[128,2048]{0,1:T(8,128)(2,1)S(1)}, u32[]{:S(2)}, u32[]{:S(2)}) collective-permute-start(bf16[128,2048]{0,1:T(8,128)(2,1)S(1)} %pad_maximum_fusion.1), channel_id=1, source_target_pairs={{0,1},{1,2},{2,3},{3,4},{4,5},{5,6},{6,7},{7,8},{8,9},{9,10},{10,1... | collective-permute-start | bytes 1572872 | tf_op jit(solution)/shard_map/ppermute | solution.py:22
  196.6 19.3 %all-gather.2 = f32[64,512]{1,0:T(8,128)S(1)} all-gather(f32[16,512]{1,0:T(8,128)S(1)} %get-tuple-element.104), channel_id=4, replica_groups=mesh['doc'=2,'coarse'=4,'fine_0'=4,'fine_1'=4] {'coarse'}, dimensions={0}, use_global_device_ids=true | all-gather | bytes 163840 | tf_op jit(solution)/shard_map/all_gather | solution.py:48
  215.9 10.7 %all_gather.51 = f32[4,16,512]{2,1,0:T(8,128)S(1)} all-gather(f32[1,16,512]{2,1,0:T(8,128)S(1)} %get-tuple-element.242), channel_id=1, replica_groups=mesh['doc'=2,'coarse'=4,'fine_0'=4,'fine_1'=4] {'fine_0'}, dimensions={0}, use_global_device_ids=true | all-gather | bytes 163840 | tf_op jit(solution)/shard_map/all_gather | solution.py:48
  226.6 10.7 %all_gather.56 = f32[4,16,512]{2,1,0:T(8,128)S(1)} all-gather(f32[1,16,512]{2,1,0:T(8,128)S(1)} %get-tuple-element.241), channel_id=1, replica_groups=mesh['doc'=2,'coarse'=4,'fine_0'=4,'fine_1'=4] {'fine_0'}, dimensions={0}, use_global_device_ids=true | all-gather | bytes 163840 | tf_op jit(solution)/shard_map/all_gather | solution.py:48
  238.1 10.3 %all_gather.57 = f32[4,16,512]{2,1,0:T(8,128)S(1)} all-gather(f32[1,16,512]{2,1,0:T(8,128)S(1)} %get-tuple-element.239), channel_id=1, replica_groups=mesh['doc'=2,'coarse'=4,'fine_0'=4,'fine_1'=4] {'fine_1'}, dimensions={0}, use_global_device_ids=true | all-gather | bytes 163840 | tf_op jit(solution)/shard_map/all_gather | solution.py:48
  249.3 1.8 copy.50
  251.7 9.7 %all_gather.53 = f32[4,16,512]{2,1,0:T(8,128)S(1)} all-gather(f32[1,16,512]{2,1,0:T(8,128)S(1)} %get-tuple-element.240), channel_id=1, replica_groups=mesh['doc'=2,'coarse'=4,'fine_0'=4,'fine_1'=4] {'fine_1'}, dimensions={0}, use_global_device_ids=true | all-gather | bytes 163840 | tf_op jit(solution)/shard_map/all_gather | solution.py:48
  263.2 24.0 %while.40 = (s32[]{:T(128)}, f32[16,128,64]{1,2,0:T(8,128)S(1)}, bf16[16,128,64]{1,2,0:T(8,128)(2,1)}, bf16[16,384,64]{1,2,0:T(8,128)(2,1)S(1)}, bf16[16,384,64]...) while((s32[]{:T(128)}, f32[16,128,64]{1,2,0:T(8,128)S(1)}, ...), condition=%wide.region_3.4_spmd.clone.clone, body=%wide.region_0.3_spmd.clone.sunk.clone | while | flops 13172482 | bytes 745053 | solution.py:73
  263.2 1.0 fusion.151
  264.7 1.0 fusion.151
  272.2 1.0 fusion.151
  278.2 1.0 fusion.151
  279.7 1.0 fusion.151
  282.7 1.0 fusion.151
  284.2 1.0 fusion.151
  287.3 6.3 %fusion.44 = f32[1,16,512,64]{2,3,1,0:T(8,128)} fusion(f32[4,16,512,64]{2,3,1,0:T(8,128)} %all-gather.10.cloned.1.call-done, f32[16,512]{1,0:T(8,128)S(1)} %copy-done.9, f32[16,512]{1,0:T(8,128)S(1)} %copy-done.6, f32[16,512]{1,0:T(8,128)S(1)} %copy-done.8, f32[16,512]{1,0:T(8,128)S(1)} %copy-done.7, f32[16,512]{1,0:T(8,128)S(1)} %copy-done.5, ...), kind=kLoop, calls=%fused_computation.60 | loop fusion | flops 4718592 | bytes 10682368 | tf_op jit(solution)/shard_map/add | solution.py:82
  293.6 73.1 %all-gather.8.cloned.1.call-done = bf16[4096,2048]{1,0:T(8,128)(2,1)} async-done(((bf16[64,2048]{1,0:T(8,128)(2,1)}), bf16[4096,2048]{1,0:T(8,128)(2,1)}) %all-gather.8.cloned.1.call-update) | async-done | bytes 16777232 | tf_op jit(solution)/shard_map/all_gather | solution.py:115
  366.7 12.0 %fusion.107 = (bf16[4096,1024]{1,0:T(8,128)(2,1)}, bf16[4096,1024]{1,0:T(8,128)(2,1)}) fusion(bf16[4096,2048]{1,0:T(8,128)(2,1)} %all-gather.8.cloned.1.call-done), kind=kLoop, calls=%fused_computation.185 | loop fusion | bytes 33554432 | tf_op jit(solution)/shard_map/slice | solution.py:119
  378.7 11.5 %copy.67 = bf16[4096,1024]{0,1:T(8,128)(2,1)} copy(bf16[4096,1024]{1,0:T(8,128)(2,1)} %get-tuple-element.254) | data formatting | bytes 16777216
  390.2 11.4 %copy.68 = bf16[4096,1024]{0,1:T(8,128)(2,1)} copy(bf16[4096,1024]{1,0:T(8,128)(2,1)} %get-tuple-element.253) | data formatting | bytes 16777216
  401.7 59.1 %while.38 = (s32[]{:T(128)}, bf16[16,128,64]{1,2,0:T(8,128)(2,1)S(1)}, bf16[16,128,64]{1,2,0:T(8,128)(2,1)}, bf16[16,4096,64]{1,2,0:T(8,128)(2,1)}, bf16[16,4096,64]{1,2,0:T(8,128)(2,1)}) while((s32[]{:T(128)}, bf16[16,128,64]{1,2,0:T(8,128)(2,1)S(1)}, bf16[16,128,64]{1,2,0:T(8,128)(2,1)}, bf16[16,4096,64]{1,2,0:T(8,128)(2,1)}, ...), condition=%wide.region_8.9_spmd.clone, body=%wide.region_5.8_spmd.sunk.clone | while | flops 137887488 | bytes 7393861 | solution.py:73
  401.7 1.7 fusion.141
  403.8 1.6 fusion.143
  405.4 1.6 fusion.141
  407.5 1.6 fusion.143
  409.1 1.6 fusion.141
  411.2 1.6 fusion.143
  412.8 1.6 fusion.141
  414.9 1.6 fusion.143
  416.5 1.6 fusion.141
  418.6 1.6 fusion.143
  420.2 1.6 fusion.141
  422.3 1.6 fusion.143
  423.9 1.6 fusion.141
  426.0 1.6 fusion.143
  427.6 1.6 fusion.141
  429.6 1.6 fusion.143
  431.3 1.6 fusion.141
  433.3 1.6 fusion.143
  435.0 1.6 fusion.141
  437.0 1.6 fusion.143
  438.7 1.6 fusion.141
  440.7 1.6 fusion.143
  442.4 1.6 fusion.141
  444.4 1.6 fusion.143
  446.1 1.6 fusion.141
  448.1 1.6 fusion.143
  449.7 1.6 fusion.141
  451.8 1.6 fusion.143
  453.4 1.6 fusion.141
  455.5 1.6 fusion.143
  457.1 1.6 fusion.141
  459.2 1.6 fusion.143
  462.4 5.0 %fusion.58 = bf16[16,512,64]{1,2,0:T(8,128)(2,1)S(1)} fusion(f32[4,16,512,64]{2,3,1,0:T(8,128)} %all-gather.12.cloned.1.call-done, f32[16,512]{1,0:T(8,128)S(1)} %copy-done.11, f32[16,512]{1,0:T(8,128)S(1)} %copy-done.17, f32[16,512]{1,0:T(8,128)S(1)} %copy-done.16, f32[16,512]{1,0:T(8,128)S(1)} %copy-done.15, f32[16,512]{1,0:T(8,128)S(1)} %copy-done.14, ...), kind=kLoop, calls=%fused_computation.81 | loop fusion | flops 5767168 | bytes 9666560 | tf_op jit(solution)/shard_map/convert_element_type | solution.py:150
  467.4 1.3 copy.59
  (218 shorter events, 50.4 us)
Async XLA Ops:
  7.2 1.6 copy-start.18
  7.2 108.3 %all-gather.14.cloned.1.call-start = ((), (), s32[]{:S(2)}) async-start(), calls=%async_computation.4 | async-start | bytes 10485760 | tf_op jit(solution)/shard_map/all_gather | solution.py:48
  28.8 258.4 %all-gather.10.cloned.1.call-start = ((), (), s32[]{:S(2)}) async-start(), calls=%async_computation.2 | async-start | bytes 10485760 | tf_op jit(solution)/shard_map/all_gather | solution.py:48
  121.8 0.7 copy-start.19
  121.8 1.0 copy-start.3
  121.8 1.0 copy-start.4
  121.8 244.8 %all-gather.8.cloned.1.call-start = ((), (), s32[]{:S(2)}) async-start(), calls=%async_computation.1 | async-start | bytes 17039360 | tf_op jit(solution)/shard_map/all_gather | solution.py:115
  185.9 3.9 copy-start
  185.9 4.1 copy-start.1
  189.8 58.6 %copy-start.2 = (bf16[1,128,1024]{2,1,0:T(8,128)(2,1)S(1)}, bf16[1,128,1024]{2,1,0:T(8,128)(2,1)}, u32[]{:S(2)}) copy-start(bf16[1,128,1024]{2,1,0:T(8,128)(2,1)} %param.16) | copy-start | bytes 786436
  189.8 272.5 %all-gather.12.cloned.1.call-start = ((), (), s32[]{:S(2)}) async-start(), calls=%async_computation.3 | async-start | bytes 10485760 | tf_op jit(solution)/shard_map/all_gather | solution.py:48
  190.1 61.0 %copy-start.20 = (s32[1,64]{1,0:T(1,128)S(1)}, s32[1,64]{1,0:T(1,128)}, u32[]{:S(2)}) copy-start(s32[1,64]{1,0:T(1,128)} %param.24) | copy-start | bytes 772
  190.3 72.5 %collective-permute-start.1 = (bf16[128,2048]{0,1:T(8,128)(2,1)S(1)}, bf16[128,2048]{0,1:T(8,128)(2,1)S(1)}, u32[]{:S(2)}, u32[]{:S(2)}) collective-permute-start(bf16[128,2048]{0,1:T(8,128)(2,1)S(1)} %pad_maximum_fusion.1), channel_id=1, source_target_pairs={{1,0},{2,1},{3,2},{4,3},{5,4},{6,5},{7,6},{8,7},{9,8},{10,9},{11,1... | collective-permute-start | bytes 1572872 | tf_op jit(solution)/shard_map/ppermute | solution.py:23
  191.6 71.2 %collective-permute-start = (bf16[128,2048]{0,1:T(8,128)(2,1)S(1)}, bf16[128,2048]{0,1:T(8,128)(2,1)S(1)}, u32[]{:S(2)}, u32[]{:S(2)}) collective-permute-start(bf16[128,2048]{0,1:T(8,128)(2,1)S(1)} %pad_maximum_fusion.1), channel_id=1, source_target_pairs={{0,1},{1,2},{2,3},{3,4},{4,5},{5,6},{6,7},{7,8},{8,9},{9,10},{10,1... | collective-permute-start | bytes 1572872 | tf_op jit(solution)/shard_map/ppermute | solution.py:22
  263.2 24.1 %copy-start.5 = (f32[16,512]{1,0:T(8,128)S(1)}, f32[16,512]{1,0:T(8,128)}, u32[]{:S(2)}) copy-start(f32[16,512]{1,0:T(8,128)} %get-tuple-element.257) | copy-start | bytes 98308
  263.2 24.1 %copy-start.6 = (f32[16,512]{1,0:T(8,128)S(1)}, f32[16,512]{1,0:T(8,128)}, u32[]{:S(2)}) copy-start(f32[16,512]{1,0:T(8,128)} %get-tuple-element.258) | copy-start | bytes 98308
  263.2 24.1 %copy-start.7 = (f32[16,512]{1,0:T(8,128)S(1)}, f32[16,512]{1,0:T(8,128)}, u32[]{:S(2)}) copy-start(f32[16,512]{1,0:T(8,128)} %get-tuple-element.259) | copy-start | bytes 98308
  263.2 24.1 %copy-start.8 = (f32[16,512]{1,0:T(8,128)S(1)}, f32[16,512]{1,0:T(8,128)}, u32[]{:S(2)}) copy-start(f32[16,512]{1,0:T(8,128)} %get-tuple-element.260) | copy-start | bytes 98308
  263.2 24.1 %copy-start.9 = (f32[16,512]{1,0:T(8,128)S(1)}, f32[16,512]{1,0:T(8,128)}, u32[]{:S(2)}) copy-start(f32[16,512]{1,0:T(8,128)} %get-tuple-element.261) | copy-start | bytes 98308
  263.2 24.1 %copy-start.10 = (f32[16,512]{1,0:T(8,128)S(1)}, f32[16,512]{1,0:T(8,128)}, u32[]{:S(2)}) copy-start(f32[16,512]{1,0:T(8,128)} %get-tuple-element.243) | copy-start | bytes 98308
  401.6 60.7 %copy-start.11 = (f32[16,512]{1,0:T(8,128)S(1)}, f32[16,512]{1,0:T(8,128)}, u32[]{:S(2)}) copy-start(f32[16,512]{1,0:T(8,128)} %get-tuple-element.232) | copy-start | bytes 98308
  401.6 60.7 %copy-start.12 = (f32[16,512]{1,0:T(8,128)S(1)}, f32[16,512]{1,0:T(8,128)}, u32[]{:S(2)}) copy-start(f32[16,512]{1,0:T(8,128)} %get-tuple-element.233) | copy-start | bytes 98308
  401.6 60.7 %copy-start.13 = (f32[16,512]{1,0:T(8,128)S(1)}, f32[16,512]{1,0:T(8,128)}, u32[]{:S(2)}) copy-start(f32[16,512]{1,0:T(8,128)} %get-tuple-element.234) | copy-start | bytes 98308
  401.6 60.7 %copy-start.14 = (f32[16,512]{1,0:T(8,128)S(1)}, f32[16,512]{1,0:T(8,128)}, u32[]{:S(2)}) copy-start(f32[16,512]{1,0:T(8,128)} %get-tuple-element.235) | copy-start | bytes 98308
  401.6 60.7 %copy-start.15 = (f32[16,512]{1,0:T(8,128)S(1)}, f32[16,512]{1,0:T(8,128)}, u32[]{:S(2)}) copy-start(f32[16,512]{1,0:T(8,128)} %get-tuple-element.236) | copy-start | bytes 98308
  401.6 60.7 %copy-start.16 = (f32[16,512]{1,0:T(8,128)S(1)}, f32[16,512]{1,0:T(8,128)}, u32[]{:S(2)}) copy-start(f32[16,512]{1,0:T(8,128)} %get-tuple-element.237) | copy-start | bytes 98308
  401.6 60.7 %copy-start.17 = (f32[16,512]{1,0:T(8,128)S(1)}, f32[16,512]{1,0:T(8,128)}, u32[]{:S(2)}) copy-start(f32[16,512]{1,0:T(8,128)} %get-tuple-element.238) | copy-start | bytes 98308
Sparse Core Ops, SparseCore 0:
  28.9 86.5 all-gather.13
  122.0 138.5 all-gather.9
  263.4 103.2 all-gather.7
  368.2 82.6 all-gather.11
where the time goes:
time: 478 us; the launch traced here: 475 us
  waiting for transfers between devices  148 us (31%)
  blocking collectives  134 us (28%)
  matrix products  88.7 us (19%)
  local copies, waits for them, and re-layouts  44.7 us (9%)
  other arithmetic  37.9 us (8%)
  between operations  14.2 us (3%)
  starting transfers between devices  6.46 us (1%)
    all_gather x3, waiting for transfers between devices, joined_all(): pieces = jax.tree.map(lambda part: lax.all_gather(part, axis), value)  75 us
    all_gather x1, waiting for transfers between devices, local(): keys_all = lax.all_gather(share, COARSE_FINE, axis=0, tiled=True)  73.1 us
    all_gather x6, blocking collectives, joined_all(): pieces = jax.tree.map(lambda part: lax.all_gather(part, axis), value)  72.3 us
    all_to_all x1, blocking collectives, sum_at_owner(): lax.all_to_all(pieces, axis, split_axis=0, concat_axis=0, tiled=True)  61.8 us
    dot_general x32, matrix products, one_head(): jnp.dot(qa, ka.T, preferred_element_type=jnp.float32) * HEAD ** (-0.5)  42.1 us
    unnamed x51, local copies, waits for them, and re-layouts  30.5 us
    dot_general x32, matrix products, one_head(): return jnp.dot(weights, va, preferred_element_type=jnp.float32)  30 us
    dot_general x16, matrix products, partial_head(): jnp.dot(weights.astype(jnp.bfloat16), enc_values, preferred_element_type=...  13.8 us
  transfers between devices with their start and end apart: 6, of which 2 were waited for; matrix products, arithmetic and copies ran while one was open for 29% of the time, Pallas kernels for 0%

commit v1 on v0

--- a/solution.py
+++ b/solution.py
@@ -112,7 +112,9 @@
         "sb,bre->sre", pick_keys, heavy_kv, preferred_element_type=jnp.float32
     ).reshape(KGRP * ROUTED_BLOCK, 2 * width)
     share = sum_at_owner(slots.astype(jnp.bfloat16), FINE, 0).astype(jnp.bfloat16)
-    keys_all = lax.all_gather(share, COARSE_FINE, axis=0, tiled=True)
+    keys_all = jnp.concatenate(
+        lax.all_to_all(jnp.stack([share] * lax.axis_size(COARSE_FINE)), COARSE_FINE, 0, 0), axis=0
+    )
     query_group = lax.dynamic_slice_in_dim(query_ids[0], group * n_fine, n_fine)
     pick_rows = (query_group[:, None] == mine[None, :]).astype(jnp.bfloat16)
     heavy_query = q_heavy[0]

time: 478 us -> 564 us (1.18)
  the two profiles are of different devices: /device:TPU:1 before, /device:TPU:66 now
where the time goes in v1:
time: 564 us; the launch traced here: 561 us
  blocking collectives  354 us (63%)
  matrix products  88.7 us (16%)
  local copies, waits for them, and re-layouts  52.2 us (9%)
  other arithmetic  37.1 us (7%)
  between operations  14.2 us (3%)
  starting transfers between devices  13.9 us (2%)
    all_gather x6, blocking collectives, joined_all(): pieces = jax.tree.map(lambda part: lax.all_gather(part, axis), value)  297 us
    all_to_all x1, blocking collectives, sum_at_owner(): lax.all_to_all(pieces, axis, split_axis=0, concat_axis=0, tiled=True)  56.9 us
    dot_general x32, matrix products, one_head(): jnp.dot(qa, ka.T, preferred_element_type=jnp.float32) * HEAD ** (-0.5)  42 us
    dot_general x32, matrix products, one_head(): return jnp.dot(weights, va, preferred_element_type=jnp.float32)  30 us
    slice x2, local copies, waits for them, and re-layouts, local(): keys_all[:, width:]  24.1 us
    dot_general x16, matrix products, partial_head(): jnp.dot(weights.astype(jnp.bfloat16), enc_values, preferred_element_type=...  13.9 us
    add x2, other arithmetic, combine(): leading_entry[2] * scale_a[..., None] + second[2] * scale_b[..., None]  12.6 us
    slice x1, local copies, waits for them, and re-layouts, local(): keys_all[:, :width]  11.3 us
  transfers between devices with their start and end apart: 6, of which 0 were waited for; matrix products, arithmetic and copies ran while one was open for 26% of the time, Pallas kernels for 0%

profile of v1, /device:TPU:66, one launch (start us, length us, event | category | flops | bytes accessed | tf_op | source)
XLA Modules:
  0.0 561.2 jit_solution(1260505417491260971)
XLA Ops:
  7.2 1.5 copy.72
  8.8 20.0 %while.39 = (s32[]{:T(128)}, f32[16,512]{1,0:T(8,128)S(1)}, f32[16,512]{1,0:T(8,128)S(1)}, f32[16,512,64]{1,2,0:T(8,128)}, bf16[16,512,64]{1,2,0:T(8,128)(2,1)S(...) while((s32[]{:T(128)}, f32[16,512]{1,0:T(8,128)S(1)}, ...), condition=%wide.region_13.14_spmd.clone, body=%wide.region_10.13_spmd.sunk.clone | while | flops 17169408 | bytes 1048677 | solution.py:146
  30.0 1.2 multiply_convert_fusion
  31.2 56.9 %all_to_all.10 = bf16[16,64,2048]{2,1,0:T(8,128)(2,1)} all-to-all(bf16[16,64,2048]{2,1,0:T(8,128)(2,1)S(1)} %bitcast.388), channel_id=1, replica_groups=mesh['doc'=2,'coarse'=4,'fine_0'=4,'fine_1'=4] {'fine_0','fine_1'}, dimensions={0} | all-to-all | bytes 8388608 | tf_op jit(solution)/shard_map/all_to_all | solution.py:42
  88.1 3.0 reduce_sum.48
  91.1 6.0 %stack.2 = bf16[64,64,2048]{2,1,0:T(8,128)(2,1)} broadcast(bf16[64,2048]{1,0:T(8,128)(2,1)S(1)} %reduce_sum.48), dimensions={1,2} | broadcast | bytes 17039360 | tf_op jit(solution)/shard_map/stack | solution.py:116
  97.1 8.0 %all-to-all-start.1 = ((bf16[64,64,2048]{2,1,0:T(8,128)(2,1)}), bf16[64,64,2048]{2,1,0:T(8,128)(2,1)}, u32[]{:S(2)}, u32[]{:S(2)}) async-start(bf16[64,64,2048]{2,1,0:T(8,128)(2,1)} %stack.2), calls=%async_computation.1 | async-start | bytes 33554432 | tf_op jit(solution)/shard_map/all_to_all | solution.py:116
  105.2 144.3 %all-gather.1 = f32[64,512]{1,0:T(8,128)S(1)} all-gather(f32[16,512]{1,0:T(8,128)S(1)} %get-tuple-element.103), channel_id=3, replica_groups=mesh['doc'=2,'coarse'=4,'fine_0'=4,'fine_1'=4] {'coarse'}, dimensions={0}, use_global_device_ids=true | all-gather | bytes 163840 | tf_op jit(solution)/shard_map/all_gather | solution.py:48
  249.6 6.3 %fusion.50 = f32[1,16,512,64]{2,3,1,0:T(8,128)} fusion(f32[64,512,64]{1,2,0:T(8,128)} %all-gather.11.cloned.1.call-done, f32[16,512]{1,0:T(8,128)S(1)} %get-tuple-element.288, f32[16,512]{1,0:T(8,128)S(1)} %get-tuple-element.285, f32[16,512]{1,0:T(8,128)S(1)} %get-tuple-element.287, f32[16,512]{1,0:T(8,128)S(1)} %get-tuple-element.286, ...), kind=kLoop, calls=%fused_computation.70 | loop fusion | flops 4718592 | bytes 10682368 | tf_op jit(solution)/shard_map/add | solution.py:82
  257.2 1.9 collective-permute-start.1
  259.2 3.9 collective-permute-start
  263.1 30.1 %all-gather.2 = f32[64,512]{1,0:T(8,128)S(1)} all-gather(f32[16,512]{1,0:T(8,128)S(1)} %get-tuple-element.104), channel_id=4, replica_groups=mesh['doc'=2,'coarse'=4,'fine_0'=4,'fine_1'=4] {'coarse'}, dimensions={0}, use_global_device_ids=true | all-gather | bytes 163840 | tf_op jit(solution)/shard_map/all_gather | solution.py:48
  293.2 49.8 %all_gather.47 = f32[4,16,512]{2,1,0:T(8,128)S(1)} all-gather(f32[1,16,512]{2,1,0:T(8,128)S(1)} %get-tuple-element.264), channel_id=1, replica_groups=mesh['doc'=2,'coarse'=4,'fine_0'=4,'fine_1'=4] {'fine_0'}, dimensions={0}, use_global_device_ids=true | all-gather | bytes 163840 | tf_op jit(solution)/shard_map/all_gather | solution.py:48
  343.0 12.8 %all_gather.52 = f32[4,16,512]{2,1,0:T(8,128)S(1)} all-gather(f32[1,16,512]{2,1,0:T(8,128)S(1)} %get-tuple-element.263), channel_id=1, replica_groups=mesh['doc'=2,'coarse'=4,'fine_0'=4,'fine_1'=4] {'fine_0'}, dimensions={0}, use_global_device_ids=true | all-gather | bytes 163840 | tf_op jit(solution)/shard_map/all_gather | solution.py:48
  356.6 47.8 %all_gather.53 = f32[4,16,512]{2,1,0:T(8,128)S(1)} all-gather(f32[1,16,512]{2,1,0:T(8,128)S(1)} %get-tuple-element.261), channel_id=1, replica_groups=mesh['doc'=2,'coarse'=4,'fine_0'=4,'fine_1'=4] {'fine_1'}, dimensions={0}, use_global_device_ids=true | all-gather | bytes 163840 | tf_op jit(solution)/shard_map/all_gather | solution.py:48
  405.2 1.8 copy.66
  407.7 12.2 %all_gather.49 = f32[4,16,512]{2,1,0:T(8,128)S(1)} all-gather(f32[1,16,512]{2,1,0:T(8,128)S(1)} %get-tuple-element.262), channel_id=1, replica_groups=mesh['doc'=2,'coarse'=4,'fine_0'=4,'fine_1'=4] {'fine_1'}, dimensions={0}, use_global_device_ids=true | all-gather | bytes 163840 | tf_op jit(solution)/shard_map/all_gather | solution.py:48
  421.7 23.9 %while.40 = (s32[]{:T(128)}, f32[16,128,64]{1,2,0:T(8,128)S(1)}, bf16[16,128,64]{1,2,0:T(8,128)(2,1)}, bf16[16,384,64]{1,2,0:T(8,128)(2,1)S(1)}, bf16[16,384,64]...) while((s32[]{:T(128)}, f32[16,128,64]{1,2,0:T(8,128)S(1)}, ...), condition=%wide.region_3.4_spmd.clone.clone, body=%wide.region_0.3_spmd.clone.sunk.clone | while | flops 13172482 | bytes 745053 | solution.py:73
  421.7 1.0 fusion.151
  424.8 1.0 fusion.151
  427.7 1.0 fusion.151
  429.2 1.0 fusion.151
  430.7 1.0 fusion.151
  432.2 1.0 fusion.151
  433.7 1.0 fusion.151
  445.8 6.3 %fusion.44 = f32[1,16,512,64]{2,3,1,0:T(8,128)} fusion(f32[4,16,512,64]{2,3,1,0:T(8,128)} %all-gather.7.cloned.1.call-done, f32[16,512]{1,0:T(8,128)S(1)} %copy-done.9, f32[16,512]{1,0:T(8,128)S(1)} %copy-done.6, f32[16,512]{1,0:T(8,128)S(1)} %copy-done.8, f32[16,512]{1,0:T(8,128)S(1)} %copy-done.7, f32[16,512]{1,0:T(8,128)S(1)} %copy-done.5, ...), kind=kLoop, calls=%fused_computation.60 | loop fusion | flops 4718592 | bytes 10682368 | tf_op jit(solution)/shard_map/add | solution.py:82
  452.1 12.2 %fusion.107 = (bf16[4096,1024]{1,0:T(8,128)(2,1)}, bf16[4096,1024]{1,0:T(8,128)(2,1)}) fusion(bf16[4096,2048]{1,0:T(8,128)(2,1)} %bitcast.22), kind=kLoop, calls=%fused_computation.185 | loop fusion | bytes 33554432 | tf_op jit(solution)/shard_map/slice | solution.py:121
  464.3 11.3 %copy.67 = bf16[4096,1024]{0,1:T(8,128)(2,1)} copy(bf16[4096,1024]{1,0:T(8,128)(2,1)} %get-tuple-element.276) | data formatting | bytes 16777216 | tf_op jit(solution)/shard_map/slice | solution.py:121
  475.6 11.9 %copy.68 = bf16[4096,1024]{0,1:T(8,128)(2,1)} copy(bf16[4096,1024]{1,0:T(8,128)(2,1)} %get-tuple-element.275) | data formatting | bytes 16777216 | tf_op jit(solution)/shard_map/slice | solution.py:121
  487.6 59.1 %while.38 = (s32[]{:T(128)}, bf16[16,128,64]{1,2,0:T(8,128)(2,1)S(1)}, bf16[16,128,64]{1,2,0:T(8,128)(2,1)}, bf16[16,4096,64]{1,2,0:T(8,128)(2,1)}, bf16[16,4096,64]{1,2,0:T(8,128)(2,1)}) while((s32[]{:T(128)}, bf16[16,128,64]{1,2,0:T(8,128)(2,1)S(1)}, bf16[16,128,64]{1,2,0:T(8,128)(2,1)}, bf16[16,4096,64]{1,2,0:T(8,128)(2,1)}, ...), condition=%wide.region_8.9_spmd.clone, body=%wide.region_5.8_spmd.sunk.clone | while | flops 137887488 | bytes 7393861 | solution.py:73
  487.6 1.6 fusion.141
  489.7 1.6 fusion.143
  491.4 1.6 fusion.141
  493.4 1.6 fusion.143
  495.1 1.6 fusion.141
  497.1 1.6 fusion.143
  498.8 1.6 fusion.141
  500.8 1.6 fusion.143
  502.5 1.6 fusion.141
  504.5 1.6 fusion.143
  506.2 1.6 fusion.141
  508.2 1.6 fusion.143
  509.9 1.6 fusion.141
  511.9 1.6 fusion.143
  513.6 1.6 fusion.141
  515.6 1.6 fusion.143
  517.3 1.6 fusion.141
  519.3 1.6 fusion.143
  521.0 1.6 fusion.141
  523.0 1.6 fusion.143
  524.6 1.6 fusion.141
  526.7 1.6 fusion.143
  528.3 1.6 fusion.141
  530.4 1.6 fusion.143
  532.0 1.6 fusion.141
  534.1 1.6 fusion.143
  535.7 1.6 fusion.141
  537.7 1.6 fusion.143
  539.4 1.6 fusion.141
  541.4 1.6 fusion.143
  543.1 1.6 fusion.141
  545.1 1.6 fusion.143
  548.4 5.0 fusion.58
  553.4 1.3 copy.75
  (218 shorter events, 51.5 us)
Async XLA Ops:
  7.2 1.6 copy-start.18
  7.2 242.4 %all-gather.11.cloned.1.call-start = ((), (), s32[]{:S(2)}) async-start(), calls=%async_computation.4 | async-start | bytes 10485760 | tf_op jit(solution)/shard_map/all_gather | solution.py:48
  28.8 0.7 copy-start.19
  28.8 1.0 copy-start.3
  28.8 1.0 copy-start.4
  97.1 355.0 %all-to-all-start.1 = ((bf16[64,64,2048]{2,1,0:T(8,128)(2,1)}), bf16[64,64,2048]{2,1,0:T(8,128)(2,1)}, u32[]{:S(2)}, u32[]{:S(2)}) async-start(bf16[64,64,2048]{2,1,0:T(8,128)(2,1)} %stack.2), calls=%async_computation.1 | async-start | bytes 33554432 | tf_op jit(solution)/shard_map/all_to_all | solution.py:116
  105.1 340.6 %all-gather.7.cloned.1.call-start = ((), (), s32[]{:S(2)}) async-start(), calls=%async_computation.2 | async-start | bytes 10485760 | tf_op jit(solution)/shard_map/all_gather | solution.py:48
  255.9 0.9 copy-start
  255.9 1.1 copy-start.1
  255.9 148.5 %copy-start.2 = (bf16[1,128,1024]{2,1,0:T(8,128)(2,1)S(1)}, bf16[1,128,1024]{2,1,0:T(8,128)(2,1)}, u32[]{:S(2)}) copy-start(bf16[1,128,1024]{2,1,0:T(8,128)(2,1)} %param.16) | copy-start | bytes 786436
  255.9 292.4 %all-gather.9.cloned.1.call-start = ((), (), s32[]{:S(2)}) async-start(), calls=%async_computation.3 | async-start | bytes 10485760 | tf_op jit(solution)/shard_map/all_gather | solution.py:48
  257.0 150.0 %copy-start.20 = (s32[1,64]{1,0:T(1,128)S(1)}, s32[1,64]{1,0:T(1,128)}, u32[]{:S(2)}) copy-start(s32[1,64]{1,0:T(1,128)} %param.24) | copy-start | bytes 772
  257.2 164.1 %collective-permute-start.1 = (bf16[128,2048]{0,1:T(8,128)(2,1)S(1)}, bf16[128,2048]{0,1:T(8,128)(2,1)S(1)}, u32[]{:S(2)}, u32[]{:S(2)}) collective-permute-start(bf16[128,2048]{0,1:T(8,128)(2,1)S(1)} %pad_maximum_fusion.1), channel_id=1, source_target_pairs={{1,0},{2,1},{3,2},{4,3},{5,4},{6,5},{7,6},{8,7},{9,8},{10,9},{11,1... | collective-permute-start | bytes 1572872 | tf_op jit(solution)/shard_map/ppermute | solution.py:23
  259.2 162.1 %collective-permute-start = (bf16[128,2048]{0,1:T(8,128)(2,1)S(1)}, bf16[128,2048]{0,1:T(8,128)(2,1)S(1)}, u32[]{:S(2)}, u32[]{:S(2)}) collective-permute-start(bf16[128,2048]{0,1:T(8,128)(2,1)S(1)} %pad_maximum_fusion.1), channel_id=1, source_target_pairs={{0,1},{1,2},{2,3},{3,4},{4,5},{5,6},{6,7},{7,8},{8,9},{9,10},{10,1... | collective-permute-start | bytes 1572872 | tf_op jit(solution)/shard_map/ppermute | solution.py:22
  421.7 24.0 %copy-start.5 = (f32[16,512]{1,0:T(8,128)S(1)}, f32[16,512]{1,0:T(8,128)}, u32[]{:S(2)}) copy-start(f32[16,512]{1,0:T(8,128)} %get-tuple-element.279) | copy-start | bytes 98308
  421.7 24.0 %copy-start.6 = (f32[16,512]{1,0:T(8,128)S(1)}, f32[16,512]{1,0:T(8,128)}, u32[]{:S(2)}) copy-start(f32[16,512]{1,0:T(8,128)} %get-tuple-element.280) | copy-start | bytes 98308
  421.7 24.0 %copy-start.7 = (f32[16,512]{1,0:T(8,128)S(1)}, f32[16,512]{1,0:T(8,128)}, u32[]{:S(2)}) copy-start(f32[16,512]{1,0:T(8,128)} %get-tuple-element.281) | copy-start | bytes 98308
  421.7 24.0 %copy-start.8 = (f32[16,512]{1,0:T(8,128)S(1)}, f32[16,512]{1,0:T(8,128)}, u32[]{:S(2)}) copy-start(f32[16,512]{1,0:T(8,128)} %get-tuple-element.282) | copy-start | bytes 98308
  421.7 24.0 %copy-start.9 = (f32[16,512]{1,0:T(8,128)S(1)}, f32[16,512]{1,0:T(8,128)}, u32[]{:S(2)}) copy-start(f32[16,512]{1,0:T(8,128)} %get-tuple-element.283) | copy-start | bytes 98308
  421.7 24.0 %copy-start.10 = (f32[16,512]{1,0:T(8,128)S(1)}, f32[16,512]{1,0:T(8,128)}, u32[]{:S(2)}) copy-start(f32[16,512]{1,0:T(8,128)} %get-tuple-element.265) | copy-start | bytes 98308
  487.6 60.8 %copy-start.11 = (f32[16,512]{1,0:T(8,128)S(1)}, f32[16,512]{1,0:T(8,128)}, u32[]{:S(2)}) copy-start(f32[16,512]{1,0:T(8,128)} %get-tuple-element.254) | copy-start | bytes 98308
  487.6 60.8 %copy-start.12 = (f32[16,512]{1,0:T(8,128)S(1)}, f32[16,512]{1,0:T(8,128)}, u32[]{:S(2)}) copy-start(f32[16,512]{1,0:T(8,128)} %get-tuple-element.255) | copy-start | bytes 98308
  487.6 60.8 %copy-start.13 = (f32[16,512]{1,0:T(8,128)S(1)}, f32[16,512]{1,0:T(8,128)}, u32[]{:S(2)}) copy-start(f32[16,512]{1,0:T(8,128)} %get-tuple-element.256) | copy-start | bytes 98308
  487.6 60.8 %copy-start.14 = (f32[16,512]{1,0:T(8,128)S(1)}, f32[16,512]{1,0:T(8,128)}, u32[]{:S(2)}) copy-start(f32[16,512]{1,0:T(8,128)} %get-tuple-element.257) | copy-start | bytes 98308
  487.6 60.8 %copy-start.15 = (f32[16,512]{1,0:T(8,128)S(1)}, f32[16,512]{1,0:T(8,128)}, u32[]{:S(2)}) copy-start(f32[16,512]{1,0:T(8,128)} %get-tuple-element.258) | copy-start | bytes 98308
  487.6 60.8 %copy-start.16 = (f32[16,512]{1,0:T(8,128)S(1)}, f32[16,512]{1,0:T(8,128)}, u32[]{:S(2)}) copy-start(f32[16,512]{1,0:T(8,128)} %get-tuple-element.259) | copy-start | bytes 98308
  487.6 60.8 %copy-start.17 = (f32[16,512]{1,0:T(8,128)S(1)}, f32[16,512]{1,0:T(8,128)}, u32[]{:S(2)}) copy-start(f32[16,512]{1,0:T(8,128)} %get-tuple-element.260) | copy-start | bytes 98308
Sparse Core Ops, SparseCore 0:
  29.0 172.9 all-gather.10
  256.0 151.7 all-gather.6
  452.2 82.5 all-gather.8
